TPU v7x, 32 devices: a whole 2x2x4 slice. The times are simulated.
32 devices in a mesh: frame: 4 (over y, x), row: 8 (over z, core).
Axes of the slice: x: 2, y: 2, z: 4, core: 2. Of those that a mesh axis runs over, the one named last changes fastest.
Arguments:
- frames_in: bfloat16 [8, 32, 32, 256], P('frame', 'row'), may hold values from -6 to 6
- conv_first: bfloat16 [3, 3, 256, 256], replicated, may hold values from -0.125 to 0.125
- conv_second: bfloat16 [3, 3, 256, 256], replicated, may hold values from -0.125 to 0.125
- time_kernel: bfloat16 [3, 256, 256], replicated, may hold values from -0.21875 to 0.21875
- norm_gain: float32 [256], replicated, may hold values from 0.1 to 1.9
- w_query: bfloat16 [256, 256], replicated, may hold values from -0.375 to 0.375
- w_key: bfloat16 [256, 256], replicated, may hold values from -0.375 to 0.375
- w_value: bfloat16 [256, 256], replicated, may hold values from -0.375 to 0.375
- w_out: bfloat16 [256, 256], replicated, may hold values from -0.375 to 0.375
- frame_bias: float32 [8, 8], replicated, may hold values from -6 to 400
- conv_third: bfloat16 [3, 3, 256, 256], replicated, may hold values from -0.125 to 0.125
Outputs:
- encoded: bfloat16 [8, 32, 32, 256], P(None, 'row', 'frame')
All inputs are finite; a program needn't handle non-finite values.
Results may differ from a plain program's by a relative error of at most 0.018.
Values may be sent and summed in bfloat16 or wider, within the bound.
A program may use at most 64 MiB of HBM per device.

v0:
```python
import math
import jax
import jax.numpy as jnp
from jax import lax
from jax.sharding import PartitionSpec as P


def extended(cells, sides, width):
    for axis, dim in sides:
        count = lax.axis_size(axis)
        ends = count - 1
        head = lax.slice_in_dim(cells, 0, width, axis=dim)
        tail = lax.slice_in_dim(cells, cells.shape[dim] - width, cells.shape[dim], axis=dim)
        cells = jnp.concatenate(
            [
                lax.ppermute(tail, axis, [(i, (i + 1) % count) for i in range(ends)]),
                cells,
                lax.ppermute(head, axis, [((i + 1) % count, i) for i in range(ends)]),
            ],
            axis=dim,
        )
    return cells


def spatial(padded, weight, row_count, col_count):
    channels = weight.shape[2]
    summed = jnp.zeros((padded.shape[0] * row_count * col_count, weight.shape[3]), jnp.float32)
    for row_tap in range(3):
        for col_tap in range(3):
            window = padded[:, row_tap : row_tap + row_count, col_tap : col_tap + col_count, :]
            summed = summed + jnp.dot(
                window.reshape(-1, channels),
                weight[row_tap, col_tap],
                preferred_element_type=jnp.float32,
            )
    return summed.reshape(padded.shape[0], row_count, col_count, weight.shape[3])


def pad_columns(field):
    return jnp.pad(field, ((0, 0), (0, 0), (1, 1), (0, 0)))


def temporal(moved, time_kernel, norm_gain, w_query, w_key, w_value, w_out, frame_bias):
    frame_count = moved.shape[0]
    channels = moved.shape[-1]
    pixels = moved.reshape(frame_count, -1, channels)
    padded = jnp.pad(pixels, ((1, 1), (0, 0), (0, 0)))
    summed = pixels.astype(jnp.float32)
    for tap in range(3):
        shifted = padded[tap : tap + frame_count].reshape(-1, channels)
        summed = summed + jnp.dot(
            shifted, time_kernel[tap], preferred_element_type=jnp.float32
        ).reshape(pixels.shape)
    timed = summed.astype(jnp.bfloat16)
    widened = timed.astype(jnp.float32)
    scale_inv = lax.rsqrt(jnp.mean(widened * widened, axis=-1, keepdims=True) + 1e-06)
    normed = (widened * scale_inv * norm_gain).astype(jnp.bfloat16).reshape(-1, channels)
    queries = (
        jnp.dot(normed, w_query, preferred_element_type=jnp.float32)
        .astype(jnp.bfloat16)
        .reshape(pixels.shape)
    )
    key_rows = (
        jnp.dot(normed, w_key, preferred_element_type=jnp.float32)
        .astype(jnp.bfloat16)
        .reshape(pixels.shape)
    )
    value_rows = (
        jnp.dot(normed, w_value, preferred_element_type=jnp.float32)
        .astype(jnp.bfloat16)
        .reshape(pixels.shape)
    )
    scores = jnp.einsum(
        "fpc,gpc->pfg", queries, key_rows, preferred_element_type=jnp.float32
    ) / math.sqrt(channels)
    scores = scores + frame_bias
    peak = jnp.max(scores, axis=-1, keepdims=True)
    raised = jnp.exp(scores - peak)
    probs = (raised / jnp.sum(raised, axis=-1, keepdims=True)).astype(jnp.bfloat16)
    context = jnp.einsum(
        "pfg,gpc->fpc", probs, value_rows, preferred_element_type=jnp.float32
    ).astype(jnp.bfloat16)
    projected = jnp.dot(
        context.reshape(-1, channels), w_out, preferred_element_type=jnp.float32
    ).reshape(pixels.shape)
    return (widened + projected).astype(jnp.bfloat16).reshape(moved.shape)


def on_device(
    frames_in,
    conv_first,
    conv_second,
    time_kernel,
    norm_gain,
    w_query,
    w_key,
    w_value,
    w_out,
    frame_bias,
    conv_third,
):
    row_count = frames_in.shape[1]
    col_whole = frames_in.shape[2]
    haloed = extended(frames_in, (("row", 1),), 1)
    first = jax.nn.silu(spatial(pad_columns(haloed), conv_first, row_count, col_whole)).astype(
        jnp.bfloat16
    )
    haloed_two = extended(first, (("row", 1),), 1)
    second = jax.nn.silu(
        spatial(pad_columns(haloed_two), conv_second, row_count, col_whole)
    ).astype(jnp.bfloat16)
    moved = lax.all_to_all(second, "frame", split_axis=2, concat_axis=0, tiled=True)
    attended = temporal(moved, time_kernel, norm_gain, w_query, w_key, w_value, w_out, frame_bias)
    col_count = attended.shape[2]
    framed_last = extended(attended, (("frame", 2), ("row", 1)), 1)
    return spatial(framed_last, conv_third, row_count, col_count).astype(jnp.bfloat16)


def solution(mesh):
    placed = (P("frame", "row", None, None), P(), P(), P(), P(), P(), P(), P(), P(), P(), P())
    return jax.shard_map(
        on_device,
        mesh=mesh,
        in_specs=placed,
        out_specs=P(None, "row", "frame", None),
        check_vma=False,
    )
```

profile of v0, /device:TPU:21, one launch (start us, length us, event | category | flops | bytes accessed | tf_op | source)
XLA Modules:
  0.0 54.3 jit_solution(5470945481003135327)
XLA Ops:
  0.0 0.9 %fusion.102 = (bf16[2,1,32,256]{3,2,1,0:T(8,128)(2,1)S(1)}, bf16[2,1,32,256]{3,2,1,0:T(8,128)(2,1)S(1)}) fusion(bf16[2,4,32,256]{3,2,1,0:T(8,128)(2,1)} %param.11), kind=kLoop, calls=%fused_computation.152 | loop fusion | bytes 131072 | tf_op jit(solution)/shard_map/slice | solution.py:13
  0.9 2.6 %collective-permute-start.1 = (bf16[2,1,32,256]{3,2,1,0:T(8,128)(2,1)S(1)}, bf16[2,1,32,256]{3,2,1,0:T(8,128)(2,1)S(1)}, u32[]{:S(2)}, u32[]{:S(2)}) collective-permute-start(bf16[2,1,32,256]{3,2,1,0:T(8,128)(2,1)S(1)} %get-tuple-element.38), channel_id=1, source_target_pairs={{1,0},{2,1},{3,2},{4,3},{5,4},{6,5},{7,6},{9,8},{10,9},{11,10},{12... | collective-permute-start | bytes 98312 | tf_op jit(solution)/shard_map/ppermute | solution.py:18
  3.5 3.1 %collective-permute-start = (bf16[2,1,32,256]{3,2,1,0:T(8,128)(2,1)S(1)}, bf16[2,1,32,256]{3,2,1,0:T(8,128)(2,1)S(1)}, u32[]{:S(2)}, u32[]{:S(2)}) collective-permute-start(bf16[2,1,32,256]{3,2,1,0:T(8,128)(2,1)S(1)} %get-tuple-element.37), channel_id=1, source_target_pairs={{0,1},{1,2},{2,3},{3,4},{4,5},{5,6},{6,7},{8,9},{9,10},{10,11},{11... | collective-permute-start | bytes 98312 | tf_op jit(solution)/shard_map/ppermute | solution.py:16
  6.6 1.0 %collective-permute-done = bf16[2,1,32,256]{3,2,1,0:T(8,128)(2,1)S(1)} collective-permute-done((bf16[2,1,32,256]{3,2,1,0:T(8,128)(2,1)S(1)}, bf16[2,1,32,256]{3,2,1,0:T(8,128)(2,1)S(1)}, u32[]{:S(2)}, u32[]{:S(2)}) %collective-permute-start) | collective-permute-done | bytes 32800 | tf_op jit(solution)/shard_map/ppermute | solution.py:16
  7.6 1.0 %fusion.19 = bf16[2,6,34,256]{3,2,1,0:T(8,128)(2,1)S(1)} fusion(bf16[2,1,32,256]{3,2,1,0:T(8,128)(2,1)S(1)} %collective-permute-done.1, bf16[2,4,32,256]{3,2,1,0:T(8,128)(2,1)} %param.11, bf16[2,1,32,256]{3,2,1,0:T(8,128)(2,1)S(1)} %collective-permute-done), kind=kLoop, calls=%fused_computation.58 | loop fusion | flops 1253376 | bytes 405504 | tf_op jit(solution)/shard_map/concatenate | solution.py:14
  9.1 0.4 copy-done.1
  9.5 0.2 convolution_add_fusion.22
  9.7 0.2 convolution_add_fusion.21
  9.9 0.2 convolution_add_fusion.20
  10.1 0.2 convolution_add_fusion.19
  10.3 0.2 convolution_add_fusion.18
  10.5 0.2 convolution_add_fusion.17
  10.7 0.2 fusion.5
  11.0 3.2 %collective-permute-start.3 = (bf16[2,1,32,256]{3,2,1,0:T(8,128)(2,1)S(1)}, bf16[2,1,32,256]{3,2,1,0:T(8,128)(2,1)S(1)}, u32[]{:S(2)}, u32[]{:S(2)}) collective-permute-start(bf16[2,1,32,256]{3,2,1,0:T(8,128)(2,1)S(1)} %get-tuple-element.34), channel_id=1, source_target_pairs={{1,0},{2,1},{3,2},{4,3},{5,4},{6,5},{7,6},{9,8},{10,9},{11,10},{12... | collective-permute-start | bytes 98312 | tf_op jit(solution)/shard_map/ppermute | solution.py:18
  14.2 3.1 %collective-permute-start.2 = (bf16[2,1,32,256]{3,2,1,0:T(8,128)(2,1)S(1)}, bf16[2,1,32,256]{3,2,1,0:T(8,128)(2,1)S(1)}, u32[]{:S(2)}, u32[]{:S(2)}) collective-permute-start(bf16[2,1,32,256]{3,2,1,0:T(8,128)(2,1)S(1)} %get-tuple-element.33), channel_id=1, source_target_pairs={{0,1},{1,2},{2,3},{3,4},{4,5},{5,6},{6,7},{8,9},{9,10},{10,11},{11... | collective-permute-start | bytes 98312 | tf_op jit(solution)/shard_map/ppermute | solution.py:16
  17.3 1.0 %collective-permute-done.2 = bf16[2,1,32,256]{3,2,1,0:T(8,128)(2,1)S(1)} collective-permute-done((bf16[2,1,32,256]{3,2,1,0:T(8,128)(2,1)S(1)}, bf16[2,1,32,256]{3,2,1,0:T(8,128)(2,1)S(1)}, u32[]{:S(2)}, u32[]{:S(2)}) %collective-permute-start.2) | collective-permute-done | bytes 32800 | tf_op jit(solution)/shard_map/ppermute | solution.py:16
  18.9 0.2 convolution_add_fusion.15
  19.1 0.2 convolution_add_fusion.14
  19.3 0.2 convolution_add_fusion.13
  19.5 0.2 convolution_add_fusion.12
  19.7 0.2 convolution_add_fusion.11
  19.9 0.2 convolution_add_fusion.10
  20.1 0.2 fusion.4
  20.4 0.8 %copy.24 = bf16[2,4,32,256]{3,1,0,2:T(4,128)(2,1)} copy(bf16[2,4,32,256]{3,2,1,0:T(8,128)(2,1)S(1)} %multiply_convert_fusion.1) | data formatting | bytes 262144 | tf_op jit(solution)/shard_map/convert_element_type | solution.py:111
  21.1 3.7 %all-to-all-start = ((bf16[2,4,32,256]{3,1,0,2:T(4,128)(2,1)}), bf16[2,4,32,256]{3,1,0,2:T(4,128)(2,1)S(1)}, u32[]{:S(2)}, u32[]{:S(2)}) async-start(bf16[2,4,32,256]{3,1,0,2:T(4,128)(2,1)} %copy.24), calls=%async_computation | async-start | bytes 262144 | tf_op jit(solution)/shard_map/all_to_all | solution.py:112
  24.9 3.3 %all-to-all-done = bf16[2,4,32,256]{3,1,0,2:T(4,128)(2,1)S(1)} async-done(((bf16[2,4,32,256]{3,1,0,2:T(4,128)(2,1)}), bf16[2,4,32,256]{3,1,0,2:T(4,128)(2,1)S(1)}, u32[]{:S(2)}, u32[]{:S(2)}) %all-to-all-start) | async-done | bytes 131104 | tf_op jit(solution)/shard_map/all_to_all | solution.py:112
  28.2 0.2 fusion.34
  28.4 0.2 fusion.1
  28.6 0.3 multiply_reduce_fusion
  29.0 0.2 convolution_convert_fusion.3
  29.5 0.2 convolution_convert_fusion.2
  29.7 0.3 fusion.13
  30.0 0.3 fusion.11
  30.3 0.2 fusion.6
  30.6 2.8 %collective-permute-start.5 = (bf16[8,4,1,256]{3,2,1,0:T(2,128)(2,1)S(1)}, bf16[8,4,1,256]{3,2,1,0:T(2,128)(2,1)S(1)}, u32[]{:S(2)}, u32[]{:S(2)}) collective-permute-start(bf16[8,4,1,256]{3,2,1,0:T(2,128)(2,1)S(1)} %get-tuple-element.30), channel_id=1, source_target_pairs={{8,0},{16,8},{24,16},{9,1},{17,9},{25,17},{10,2},{18,10},{26,18},{... | collective-permute-start | bytes 49160 | tf_op jit(solution)/shard_map/ppermute | solution.py:18
  33.4 2.5 %collective-permute-start.4 = (bf16[8,4,1,256]{3,2,1,0:T(2,128)(2,1)S(1)}, bf16[8,4,1,256]{3,2,1,0:T(2,128)(2,1)S(1)}, u32[]{:S(2)}, u32[]{:S(2)}) collective-permute-start(bf16[8,4,1,256]{3,2,1,0:T(2,128)(2,1)S(1)} %get-tuple-element.29), channel_id=1, source_target_pairs={{0,8},{8,16},{16,24},{1,9},{9,17},{17,25},{2,10},{10,18},{18,26},{... | collective-permute-start | bytes 49160 | tf_op jit(solution)/shard_map/ppermute | solution.py:16
  35.9 0.2 fusion.25
  36.1 2.9 %collective-permute-done.4 = bf16[8,4,1,256]{3,2,1,0:T(2,128)(2,1)S(1)} collective-permute-done((bf16[8,4,1,256]{3,2,1,0:T(2,128)(2,1)S(1)}, bf16[8,4,1,256]{3,2,1,0:T(2,128)(2,1)S(1)}, u32[]{:S(2)}, u32[]{:S(2)}) %collective-permute-start.4) | collective-permute-done | bytes 16416 | tf_op jit(solution)/shard_map/ppermute | solution.py:16
  39.0 7.1 %collective-permute-start.6 = (bf16[8,1,10,256]{3,2,1,0:T(8,128)(2,1)S(1)}, bf16[8,1,10,256]{3,2,1,0:T(8,128)(2,1)S(1)}, u32[]{:S(2)}, u32[]{:S(2)}) collective-permute-start(bf16[8,1,10,256]{3,2,1,0:T(8,128)(2,1)S(1)} %get-tuple-element.25), channel_id=1, source_target_pairs={{0,1},{1,2},{2,3},{3,4},{4,5},{5,6},{6,7},{8,9},{9,10},{10,11},{11... | collective-permute-start | bytes 122888 | tf_op jit(solution)/shard_map/ppermute | solution.py:16
  46.1 1.9 %collective-permute-start.7 = (bf16[8,1,10,256]{3,2,1,0:T(8,128)(2,1)S(1)}, bf16[8,1,10,256]{3,2,1,0:T(8,128)(2,1)S(1)}, u32[]{:S(2)}, u32[]{:S(2)}) collective-permute-start(bf16[8,1,10,256]{3,2,1,0:T(8,128)(2,1)S(1)} %get-tuple-element.26), channel_id=1, source_target_pairs={{1,0},{2,1},{3,2},{4,3},{5,4},{6,5},{7,6},{9,8},{10,9},{11,10},{12... | collective-permute-start | bytes 122888 | tf_op jit(solution)/shard_map/ppermute | solution.py:18
  48.2 3.5 %collective-permute-done.7 = bf16[8,1,10,256]{3,2,1,0:T(8,128)(2,1)S(1)} collective-permute-done((bf16[8,1,10,256]{3,2,1,0:T(8,128)(2,1)S(1)}, bf16[8,1,10,256]{3,2,1,0:T(8,128)(2,1)S(1)}, u32[]{:S(2)}, u32[]{:S(2)}) %collective-permute-start.7) | collective-permute-done | bytes 40992 | tf_op jit(solution)/shard_map/ppermute | solution.py:18
  51.7 0.3 maximum_maximum_fusion
  52.5 0.2 convolution_add_fusion.7
  52.7 0.2 convolution_add_fusion.6
  52.9 0.2 fusion.3
  53.1 0.2 fusion.2
  53.3 0.2 convolution_add_fusion.3
  53.5 0.8 %fusion.7 = bf16[256,256]{1,0:T(8,128)(2,1)} fusion(f32[256,256]{1,0:T(8,128)S(1)} %convolution_add_fusion.3, bf16[256,256]{1,0:T(8,128)(2,1)S(1)} %bitcast.189, bf16[3,3,256,256]{3,2,1,0:T(8,128)(2,1)S(1)} %copy-done.3), kind=kOutput, calls=%fused_computation.30 | convolution fusion | flops 33685504 | bytes 655360 | tf_op jit(solution)/shard_map/dot_general | solution.py:31
  (49 shorter events, 2.6 us)
Async XLA Ops:
  0.0 29.0 %copy-start = (bf16[256,256]{1,0:T(8,128)(2,1)S(1)}, bf16[256,256]{1,0:T(8,128)(2,1)}, u32[]{:S(2)}) copy-start(bf16[256,256]{1,0:T(8,128)(2,1)} %param.18) | copy-start | bytes 393220
  0.0 8.7 %copy-start.2 = (bf16[3,3,256,256]{3,2,1,0:T(8,128)(2,1)S(1)}, bf16[3,3,256,256]{3,2,1,0:T(8,128)(2,1)}, u32[]{:S(2)}) copy-start(bf16[3,3,256,256]{3,2,1,0:T(8,128)(2,1)} %param.12) | copy-start | bytes 3538948
  0.9 5.7 %collective-permute-start.1 = (bf16[2,1,32,256]{3,2,1,0:T(8,128)(2,1)S(1)}, bf16[2,1,32,256]{3,2,1,0:T(8,128)(2,1)S(1)}, u32[]{:S(2)}, u32[]{:S(2)}) collective-permute-start(bf16[2,1,32,256]{3,2,1,0:T(8,128)(2,1)S(1)} %get-tuple-element.38), channel_id=1, source_target_pairs={{1,0},{2,1},{3,2},{4,3},{5,4},{6,5},{7,6},{9,8},{10,9},{11,10},{12... | collective-permute-start | bytes 98312 | tf_op jit(solution)/shard_map/ppermute | solution.py:18
  3.5 4.1 %collective-permute-start = (bf16[2,1,32,256]{3,2,1,0:T(8,128)(2,1)S(1)}, bf16[2,1,32,256]{3,2,1,0:T(8,128)(2,1)S(1)}, u32[]{:S(2)}, u32[]{:S(2)}) collective-permute-start(bf16[2,1,32,256]{3,2,1,0:T(8,128)(2,1)S(1)} %get-tuple-element.37), channel_id=1, source_target_pairs={{0,1},{1,2},{2,3},{3,4},{4,5},{5,6},{6,7},{8,9},{9,10},{10,11},{11... | collective-permute-start | bytes 98312 | tf_op jit(solution)/shard_map/ppermute | solution.py:16
  8.6 0.9 %copy-start.1 = (bf16[2,4,32,256]{3,2,1,0:T(8,128)(2,1)S(1)}, bf16[2,4,32,256]{3,2,1,0:T(8,128)(2,1)}, u32[]{:S(2)}) copy-start(bf16[2,4,32,256]{3,2,1,0:T(8,128)(2,1)} %param.11) | copy-start | bytes 393220
  10.9 7.6 %copy-start.4 = (bf16[3,3,256,256]{3,2,1,0:T(8,128)(2,1)S(1)}, bf16[3,3,256,256]{3,2,1,0:T(8,128)(2,1)}, u32[]{:S(2)}) copy-start(bf16[3,3,256,256]{3,2,1,0:T(8,128)(2,1)} %param.13) | copy-start | bytes 3538948
  11.0 6.3 %collective-permute-start.3 = (bf16[2,1,32,256]{3,2,1,0:T(8,128)(2,1)S(1)}, bf16[2,1,32,256]{3,2,1,0:T(8,128)(2,1)S(1)}, u32[]{:S(2)}, u32[]{:S(2)}) collective-permute-start(bf16[2,1,32,256]{3,2,1,0:T(8,128)(2,1)S(1)} %get-tuple-element.34), channel_id=1, source_target_pairs={{1,0},{2,1},{3,2},{4,3},{5,4},{6,5},{7,6},{9,8},{10,9},{11,10},{12... | collective-permute-start | bytes 98312 | tf_op jit(solution)/shard_map/ppermute | solution.py:18
  14.2 4.1 %collective-permute-start.2 = (bf16[2,1,32,256]{3,2,1,0:T(8,128)(2,1)S(1)}, bf16[2,1,32,256]{3,2,1,0:T(8,128)(2,1)S(1)}, u32[]{:S(2)}, u32[]{:S(2)}) collective-permute-start(bf16[2,1,32,256]{3,2,1,0:T(8,128)(2,1)S(1)} %get-tuple-element.33), channel_id=1, source_target_pairs={{0,1},{1,2},{2,3},{3,4},{4,5},{5,6},{6,7},{8,9},{9,10},{10,11},{11... | collective-permute-start | bytes 98312 | tf_op jit(solution)/shard_map/ppermute | solution.py:16
  20.1 4.7 %copy-start.9 = (f32[8,8]{1,0:T(8,128)S(1)}, f32[8,8]{1,0:T(8,128)}, u32[]{:S(2)}) copy-start(f32[8,8]{1,0:T(8,128)} %param.20) | copy-start | bytes 772
  20.1 8.1 %copy-start.5 = (bf16[3,256,256]{2,1,0:T(8,128)(2,1)S(1)}, bf16[3,256,256]{2,1,0:T(8,128)(2,1)}, u32[]{:S(2)}) copy-start(bf16[3,256,256]{2,1,0:T(8,128)(2,1)} %param.14) | copy-start | bytes 1179652
  21.1 7.0 %all-to-all-start = ((bf16[2,4,32,256]{3,1,0,2:T(4,128)(2,1)}), bf16[2,4,32,256]{3,1,0,2:T(4,128)(2,1)S(1)}, u32[]{:S(2)}, u32[]{:S(2)}) async-start(bf16[2,4,32,256]{3,1,0,2:T(4,128)(2,1)} %copy.24), calls=%async_computation | async-start | bytes 262144 | tf_op jit(solution)/shard_map/all_to_all | solution.py:112
  28.1 0.7 %copy-start.10 = (f32[256]{0:T(256)S(1)}, f32[256]{0:T(256)}, u32[]{:S(2)}) copy-start(f32[256]{0:T(256)} %param.15) | copy-start | bytes 3076
  28.4 0.9 %copy-start.6 = (bf16[256,256]{1,0:T(8,128)(2,1)S(1)}, bf16[256,256]{1,0:T(8,128)(2,1)}, u32[]{:S(2)}) copy-start(bf16[256,256]{1,0:T(8,128)(2,1)} %param.17) | copy-start | bytes 393220
  28.6 0.9 %copy-start.7 = (bf16[256,256]{1,0:T(8,128)(2,1)S(1)}, bf16[256,256]{1,0:T(8,128)(2,1)}, u32[]{:S(2)}) copy-start(bf16[256,256]{1,0:T(8,128)(2,1)} %param.16) | copy-start | bytes 393220
  29.3 1.0 %copy-start.8 = (bf16[256,256]{1,0:T(8,128)(2,1)S(1)}, bf16[256,256]{1,0:T(8,128)(2,1)}, u32[]{:S(2)}) copy-start(bf16[256,256]{1,0:T(8,128)(2,1)} %param.19) | copy-start | bytes 393220
  29.7 6.2 %copy-start.3 = (bf16[3,3,256,256]{3,2,1,0:T(8,128)(2,1)S(1)}, bf16[3,3,256,256]{3,2,1,0:T(8,128)(2,1)}, u32[]{:S(2)}) copy-start(bf16[3,3,256,256]{3,2,1,0:T(8,128)(2,1)} %param.21) | copy-start | bytes 3538948
  30.6 5.5 %collective-permute-start.5 = (bf16[8,4,1,256]{3,2,1,0:T(2,128)(2,1)S(1)}, bf16[8,4,1,256]{3,2,1,0:T(2,128)(2,1)S(1)}, u32[]{:S(2)}, u32[]{:S(2)}) collective-permute-start(bf16[8,4,1,256]{3,2,1,0:T(2,128)(2,1)S(1)} %get-tuple-element.30), channel_id=1, source_target_pairs={{8,0},{16,8},{24,16},{9,1},{17,9},{25,17},{10,2},{18,10},{26,18},{... | collective-permute-start | bytes 49160 | tf_op jit(solution)/shard_map/ppermute | solution.py:18
  33.4 5.6 %collective-permute-start.4 = (bf16[8,4,1,256]{3,2,1,0:T(2,128)(2,1)S(1)}, bf16[8,4,1,256]{3,2,1,0:T(2,128)(2,1)S(1)}, u32[]{:S(2)}, u32[]{:S(2)}) collective-permute-start(bf16[8,4,1,256]{3,2,1,0:T(2,128)(2,1)S(1)} %get-tuple-element.29), channel_id=1, source_target_pairs={{0,8},{8,16},{16,24},{1,9},{9,17},{17,25},{2,10},{10,18},{18,26},{... | collective-permute-start | bytes 49160 | tf_op jit(solution)/shard_map/ppermute | solution.py:16
  39.0 9.2 %collective-permute-start.6 = (bf16[8,1,10,256]{3,2,1,0:T(8,128)(2,1)S(1)}, bf16[8,1,10,256]{3,2,1,0:T(8,128)(2,1)S(1)}, u32[]{:S(2)}, u32[]{:S(2)}) collective-permute-start(bf16[8,1,10,256]{3,2,1,0:T(8,128)(2,1)S(1)} %get-tuple-element.25), channel_id=1, source_target_pairs={{0,1},{1,2},{2,3},{3,4},{4,5},{5,6},{6,7},{8,9},{9,10},{10,11},{11... | collective-permute-start | bytes 122888 | tf_op jit(solution)/shard_map/ppermute | solution.py:16
  46.1 5.6 %collective-permute-start.7 = (bf16[8,1,10,256]{3,2,1,0:T(8,128)(2,1)S(1)}, bf16[8,1,10,256]{3,2,1,0:T(8,128)(2,1)S(1)}, u32[]{:S(2)}, u32[]{:S(2)}) collective-permute-start(bf16[8,1,10,256]{3,2,1,0:T(8,128)(2,1)S(1)} %get-tuple-element.26), channel_id=1, source_target_pairs={{1,0},{2,1},{3,2},{4,3},{5,4},{6,5},{7,6},{9,8},{10,9},{11,10},{12... | collective-permute-start | bytes 122888 | tf_op jit(solution)/shard_map/ppermute | solution.py:18
where the time goes:
time: 54.8 us; the launch traced here: 54.3 us
  starting transfers between devices  29.9 us (55%)
  waiting for transfers between devices  11.6 us (21%)
  matrix products  7.61 us (14%)
  local copies, waits for them, and re-layouts  2.71 us (5%)
  other arithmetic  1.94 us (4%)
  between operations  0.57 us (1%)
    ppermute x4, starting transfers between devices, extended(): lax.ppermute(tail, axis, [(i, (i + 1) % count) for i in range(ends)])  15.8 us
    ppermute x4, starting transfers between devices, extended(): lax.ppermute(head, axis, [((i + 1) % count, i) for i in range(ends)])  10.5 us
    dot_general x27, matrix products, spatial(): jnp.dot(window.reshape(-1, channels), weight[row_tap, col_tap], preferred...  5.71 us
    ppermute x4, waiting for transfers between devices, extended(): lax.ppermute(tail, axis, [(i, (i + 1) % count) for i in range(ends)])  4.84 us
    all_to_all x1, starting transfers between devices, on_device(): lax.all_to_all(second, 'frame', split_axis=2, concat_axis=0, tiled=True)  3.67 us
    ppermute x4, waiting for transfers between devices, extended(): lax.ppermute(head, axis, [((i + 1) % count, i) for i in range(ends)])  3.52 us
    all_to_all x1, waiting for transfers between devices, on_device(): lax.all_to_all(second, 'frame', split_axis=2, concat_axis=0, tiled=True)  3.27 us
    concatenate x6, other arithmetic, extended(): jnp.concatenate([lax.ppermute(tail, axis, [(i, (i + 1) % count) for i in...  1.53 us
  transfers between devices with their start and end apart: 9, of which 5 were waited for; matrix products, arithmetic and copies ran while one was open for 1% of the time, Pallas kernels for 0%

commit v1 on v0

--- a/solution.py
+++ b/solution.py
@@ -3,6 +3,28 @@
 import jax.numpy as jnp
 from jax import lax
 from jax.sharding import PartitionSpec as P
+
+
+def cut_along(x, dim, size):
+    before, after = (x.shape[:dim], x.shape[dim + 1 :])
+    return jnp.moveaxis(x.reshape(*before, size, -1, *after), dim, 0)
+
+
+def laid_out(tiles, dim):
+    tiles = jnp.moveaxis(tiles, 0, dim)
+    shape = tiles.shape
+    return tiles.reshape(*shape[:dim], shape[dim] * shape[dim + 1], *shape[dim + 2 :])
+
+
+def exchange_directly(array, axis, split_dim, concat_dim):
+    length, index = (lax.axis_size(axis), lax.axis_index(axis))
+    parts = cut_along(array, split_dim, length)
+    done = [parts[index]]
+    for step in range(1, length):
+        sent = parts[(index + step) % length]
+        done.append(lax.ppermute(sent, axis, [(i, (i + step) % length) for i in range(length)]))
+    parts = jnp.stack(done)[(index - jnp.arange(length)) % length]
+    return laid_out(parts, concat_dim)
 
 
 def extended(cells, sides, width):
@@ -109,7 +131,7 @@
     second = jax.nn.silu(
         spatial(pad_columns(haloed_two), conv_second, row_count, col_whole)
     ).astype(jnp.bfloat16)
-    moved = lax.all_to_all(second, "frame", split_axis=2, concat_axis=0, tiled=True)
+    moved = exchange_directly(second, "frame", 2, 0)
     attended = temporal(moved, time_kernel, norm_gain, w_query, w_key, w_value, w_out, frame_bias)
     col_count = attended.shape[2]
     framed_last = extended(attended, (("frame", 2), ("row", 1)), 1)

time: 54.8 us -> 52.8 us (0.964)
  starting transfers between devices: 29.9 us -> 28.6 us
    all_to_all x1 -> x0, starting transfers between devices: 3.67 us -> none  [on_device(): lax.all_to_all(second, 'frame', split_axis=2, concat_axis=0, tiled=True)]
    ppermute x0 -> x3, waiting for transfers between devices: none -> 3.65 us  [exchange_directly(): lax.ppermute(sent, axis, [(i, (i + step) % length) for i in range(length)])]
    all_to_all x1 -> x0, waiting for transfers between devices: 3.27 us -> none  [on_device(): lax.all_to_all(second, 'frame', split_axis=2, concat_axis=0, tiled=True)]
    ppermute x0 -> x3, starting transfers between devices: none -> 2.45 us  [exchange_directly(): lax.ppermute(sent, axis, [(i, (i + step) % length) for i in range(length)])]
    ppermute x4, waiting for transfers between devices: 4.84 us -> 3.92 us  [extended(): lax.ppermute(tail, axis, [(i, (i + 1) % count) for i in range(ends)])]
    ppermute x4, starting transfers between devices: 10.5 us -> 9.59 us  [extended(): lax.ppermute(head, axis, [((i + 1) % count, i) for i in range(ends)])]
    ppermute x4, starting transfers between devices: 15.8 us -> 16.5 us  [extended(): lax.ppermute(tail, axis, [(i, (i + 1) % count) for i in range(ends)])]
    convert_element_type x1 -> x0, local copies, waits for them, and re-layouts: 0.76 us -> none  [on_device(): second = jax.nn.silu(spatial(pad_columns(haloed_two), conv_second, row_co...]
  transfers between devices with their start and end apart: 9 -> 11, of which waited for: 5 -> 7; matrix products, arithmetic and copies ran while one was open for 1% -> 1% of each run, Pallas kernels for 0% -> 0%
where the time goes in v1:
time: 52.8 us; the launch traced here: 52.4 us
  starting transfers between devices  28.6 us (54%)
  waiting for transfers between devices  11.1 us (21%)
  matrix products  7.61 us (14%)
  local copies, waits for them, and re-layouts  2.51 us (5%)
  other arithmetic  1.98 us (4%)
  between operations  0.65 us (1%)
    ppermute x4, starting transfers between devices, extended(): lax.ppermute(tail, axis, [(i, (i + 1) % count) for i in range(ends)])  16.5 us
    ppermute x4, starting transfers between devices, extended(): lax.ppermute(head, axis, [((i + 1) % count, i) for i in range(ends)])  9.59 us
    dot_general x27, matrix products, spatial(): jnp.dot(window.reshape(-1, channels), weight[row_tap, col_tap], preferred...  5.71 us
    ppermute x4, waiting for transfers between devices, extended(): lax.ppermute(tail, axis, [(i, (i + 1) % count) for i in range(ends)])  3.92 us
    ppermute x3, waiting for transfers between devices, exchange_directly(): lax.ppermute(sent, axis, [(i, (i + step) % length) for i in range(length)])  3.65 us
    ppermute x4, waiting for transfers between devices, extended(): lax.ppermute(head, axis, [((i + 1) % count, i) for i in range(ends)])  3.52 us
    ppermute x3, starting transfers between devices, exchange_directly(): lax.ppermute(sent, axis, [(i, (i + step) % length) for i in range(length)])  2.45 us
    concatenate x6, other arithmetic, extended(): jnp.concatenate([lax.ppermute(tail, axis, [(i, (i + 1) % count) for i in...  1.53 us
  transfers between devices with their start and end apart: 11, of which 7 were waited for; matrix products, arithmetic and copies ran while one was open for 1% of the time, Pallas kernels for 0%

profile of v1, /device:TPU:21, one launch (start us, length us, event | category | flops | bytes accessed | tf_op | source)
XLA Modules:
  0.0 52.4 jit_solution(13487561608668983497)
XLA Ops:
  0.0 0.9 %fusion.105 = (bf16[2,1,32,256]{3,2,1,0:T(8,128)(2,1)S(1)}, bf16[2,1,32,256]{3,2,1,0:T(8,128)(2,1)S(1)}) fusion(bf16[2,4,32,256]{3,2,1,0:T(8,128)(2,1)} %param.11), kind=kLoop, calls=%fused_computation.165 | loop fusion | bytes 131072 | tf_op jit(solution)/shard_map/slice | solution.py:35
  0.9 2.6 %collective-permute-start.1 = (bf16[2,1,32,256]{3,2,1,0:T(8,128)(2,1)S(1)}, bf16[2,1,32,256]{3,2,1,0:T(8,128)(2,1)S(1)}, u32[]{:S(2)}, u32[]{:S(2)}) collective-permute-start(bf16[2,1,32,256]{3,2,1,0:T(8,128)(2,1)S(1)} %get-tuple-element.42), channel_id=1, source_target_pairs={{1,0},{2,1},{3,2},{4,3},{5,4},{6,5},{7,6},{9,8},{10,9},{11,10},{12... | collective-permute-start | bytes 98312 | tf_op jit(solution)/shard_map/ppermute | solution.py:40
  3.5 3.1 %collective-permute-start = (bf16[2,1,32,256]{3,2,1,0:T(8,128)(2,1)S(1)}, bf16[2,1,32,256]{3,2,1,0:T(8,128)(2,1)S(1)}, u32[]{:S(2)}, u32[]{:S(2)}) collective-permute-start(bf16[2,1,32,256]{3,2,1,0:T(8,128)(2,1)S(1)} %get-tuple-element.41), channel_id=1, source_target_pairs={{0,1},{1,2},{2,3},{3,4},{4,5},{5,6},{6,7},{8,9},{9,10},{10,11},{11... | collective-permute-start | bytes 98312 | tf_op jit(solution)/shard_map/ppermute | solution.py:38
  6.6 1.0 %collective-permute-done = bf16[2,1,32,256]{3,2,1,0:T(8,128)(2,1)S(1)} collective-permute-done((bf16[2,1,32,256]{3,2,1,0:T(8,128)(2,1)S(1)}, bf16[2,1,32,256]{3,2,1,0:T(8,128)(2,1)S(1)}, u32[]{:S(2)}, u32[]{:S(2)}) %collective-permute-start) | collective-permute-done | bytes 32800 | tf_op jit(solution)/shard_map/ppermute | solution.py:38
  7.6 1.0 %fusion.18 = bf16[2,6,34,256]{3,2,1,0:T(8,128)(2,1)S(1)} fusion(bf16[2,1,32,256]{3,2,1,0:T(8,128)(2,1)S(1)} %collective-permute-done.1, bf16[2,4,32,256]{3,2,1,0:T(8,128)(2,1)} %param.11, bf16[2,1,32,256]{3,2,1,0:T(8,128)(2,1)S(1)} %collective-permute-done), kind=kLoop, calls=%fused_computation.58 | loop fusion | flops 1253376 | bytes 405504 | tf_op jit(solution)/shard_map/concatenate | solution.py:36
  9.1 0.4 copy-done.1
  9.5 0.2 convolution_add_fusion.22
  9.7 0.2 convolution_add_fusion.21
  9.9 0.2 convolution_add_fusion.20
  10.1 0.2 convolution_add_fusion.19
  10.3 0.2 convolution_add_fusion.18
  10.5 0.2 convolution_add_fusion.17
  10.7 0.2 fusion.5
  11.0 3.2 %collective-permute-start.3 = (bf16[2,1,32,256]{3,2,1,0:T(8,128)(2,1)S(1)}, bf16[2,1,32,256]{3,2,1,0:T(8,128)(2,1)S(1)}, u32[]{:S(2)}, u32[]{:S(2)}) collective-permute-start(bf16[2,1,32,256]{3,2,1,0:T(8,128)(2,1)S(1)} %get-tuple-element.38), channel_id=1, source_target_pairs={{1,0},{2,1},{3,2},{4,3},{5,4},{6,5},{7,6},{9,8},{10,9},{11,10},{12... | collective-permute-start | bytes 98312 | tf_op jit(solution)/shard_map/ppermute | solution.py:40
  14.2 3.1 %collective-permute-start.2 = (bf16[2,1,32,256]{3,2,1,0:T(8,128)(2,1)S(1)}, bf16[2,1,32,256]{3,2,1,0:T(8,128)(2,1)S(1)}, u32[]{:S(2)}, u32[]{:S(2)}) collective-permute-start(bf16[2,1,32,256]{3,2,1,0:T(8,128)(2,1)S(1)} %get-tuple-element.37), channel_id=1, source_target_pairs={{0,1},{1,2},{2,3},{3,4},{4,5},{5,6},{6,7},{8,9},{9,10},{10,11},{11... | collective-permute-start | bytes 98312 | tf_op jit(solution)/shard_map/ppermute | solution.py:38
  17.3 0.9 %collective-permute-done.2 = bf16[2,1,32,256]{3,2,1,0:T(8,128)(2,1)S(1)} collective-permute-done((bf16[2,1,32,256]{3,2,1,0:T(8,128)(2,1)S(1)}, bf16[2,1,32,256]{3,2,1,0:T(8,128)(2,1)S(1)}, u32[]{:S(2)}, u32[]{:S(2)}) %collective-permute-start.2) | collective-permute-done | bytes 32800 | tf_op jit(solution)/shard_map/ppermute | solution.py:38
  18.9 0.2 convolution_add_fusion.15
  19.1 0.2 convolution_add_fusion.14
  19.3 0.2 convolution_add_fusion.13
  19.5 0.2 convolution_add_fusion.12
  19.7 0.2 convolution_add_fusion.11
  19.9 0.2 convolution_add_fusion.10
  20.1 0.2 fusion.4
  20.4 1.2 %collective-permute-start.6 = (bf16[2,4,8,256]{3,2,1,0:T(8,128)(2,1)S(1)}, bf16[2,4,8,256]{3,2,1,0:T(8,128)(2,1)S(1)}, u32[]{:S(2)}, u32[]{:S(2)}) collective-permute-start(bf16[2,4,8,256]{3,2,1,0:T(8,128)(2,1)S(1)} %get-tuple-element.32), channel_id=1, source_target_pairs={{0,24},{8,0},{16,8},{24,16},{1,25},{9,1},{17,9},{25,17},{2,26},{10... | collective-permute-start | bytes 98312 | tf_op jit(solution)/shard_map/ppermute | solution.py:25
  21.6 1.2 %collective-permute-start.5 = (bf16[2,4,8,256]{3,2,1,0:T(8,128)(2,1)S(1)}, bf16[2,4,8,256]{3,2,1,0:T(8,128)(2,1)S(1)}, u32[]{:S(2)}, u32[]{:S(2)}) collective-permute-start(bf16[2,4,8,256]{3,2,1,0:T(8,128)(2,1)S(1)} %get-tuple-element.33), channel_id=1, source_target_pairs={{0,16},{8,24},{16,0},{24,8},{1,17},{9,25},{17,1},{25,9},{2,18},{10... | collective-permute-start | bytes 98312 | tf_op jit(solution)/shard_map/ppermute | solution.py:25
  23.0 0.3 collective-permute-done.6
  23.2 1.2 %collective-permute-done.5 = bf16[2,4,8,256]{3,2,1,0:T(8,128)(2,1)S(1)} collective-permute-done((bf16[2,4,8,256]{3,2,1,0:T(8,128)(2,1)S(1)}, bf16[2,4,8,256]{3,2,1,0:T(8,128)(2,1)S(1)}, u32[]{:S(2)}, u32[]{:S(2)}) %collective-permute-start.5) | collective-permute-done | bytes 32800 | tf_op jit(solution)/shard_map/ppermute | solution.py:25
  24.4 2.2 %collective-permute-done.4 = bf16[2,4,8,256]{3,2,1,0:T(8,128)(2,1)S(1)} collective-permute-done((bf16[2,4,8,256]{3,2,1,0:T(8,128)(2,1)S(1)}, bf16[2,4,8,256]{3,2,1,0:T(8,128)(2,1)S(1)}, u32[]{:S(2)}, u32[]{:S(2)}) %collective-permute-start.4) | collective-permute-done | bytes 32800 | tf_op jit(solution)/shard_map/ppermute | solution.py:25
  26.6 0.6 %gather_fusion = bf16[4,2,4,8,256]{4,3,2,1,0:T(8,128)(2,1)S(1)} fusion(bf16[4,2,4,8,256]{4,3,2,1,0:T(8,128)(2,1)S(1)} %pad_maximum_fusion.7, s32[1024]{0:T(1024)S(1)} %pad_clamp_fusion), kind=kCustom, calls=%fused_computation | custom fusion | bytes 262160 | tf_op jit(solution)/shard_map/gather | solution.py:26
  27.4 0.2 fusion.1
  27.6 0.3 multiply_reduce_fusion
  28.0 0.2 convolution_convert_fusion.2
  28.7 0.3 fusion.12
  29.1 0.3 fusion.60
  29.4 0.2 fusion.6
  29.6 1.9 %collective-permute-start.8 = (bf16[8,4,1,256]{3,2,1,0:T(2,128)(2,1)S(1)}, bf16[8,4,1,256]{3,2,1,0:T(2,128)(2,1)S(1)}, u32[]{:S(2)}, u32[]{:S(2)}) collective-permute-start(bf16[8,4,1,256]{3,2,1,0:T(2,128)(2,1)S(1)} %get-tuple-element.30), channel_id=1, source_target_pairs={{8,0},{16,8},{24,16},{9,1},{17,9},{25,17},{10,2},{18,10},{26,18},{... | collective-permute-start | bytes 49160 | tf_op jit(solution)/shard_map/ppermute | solution.py:40
  31.5 3.4 %collective-permute-start.7 = (bf16[8,4,1,256]{3,2,1,0:T(2,128)(2,1)S(1)}, bf16[8,4,1,256]{3,2,1,0:T(2,128)(2,1)S(1)}, u32[]{:S(2)}, u32[]{:S(2)}) collective-permute-start(bf16[8,4,1,256]{3,2,1,0:T(2,128)(2,1)S(1)} %get-tuple-element.29), channel_id=1, source_target_pairs={{0,8},{8,16},{16,24},{1,9},{9,17},{17,25},{2,10},{10,18},{18,26},{... | collective-permute-start | bytes 49160 | tf_op jit(solution)/shard_map/ppermute | solution.py:38
  35.1 2.0 %collective-permute-done.7 = bf16[8,4,1,256]{3,2,1,0:T(2,128)(2,1)S(1)} collective-permute-done((bf16[8,4,1,256]{3,2,1,0:T(2,128)(2,1)S(1)}, bf16[8,4,1,256]{3,2,1,0:T(2,128)(2,1)S(1)}, u32[]{:S(2)}, u32[]{:S(2)}) %collective-permute-start.7) | collective-permute-done | bytes 16416 | tf_op jit(solution)/shard_map/ppermute | solution.py:38
  37.2 7.0 %collective-permute-start.9 = (bf16[8,1,10,256]{3,2,1,0:T(8,128)(2,1)S(1)}, bf16[8,1,10,256]{3,2,1,0:T(8,128)(2,1)S(1)}, u32[]{:S(2)}, u32[]{:S(2)}) collective-permute-start(bf16[8,1,10,256]{3,2,1,0:T(8,128)(2,1)S(1)} %get-tuple-element.25), channel_id=1, source_target_pairs={{0,1},{1,2},{2,3},{3,4},{4,5},{5,6},{6,7},{8,9},{9,10},{10,11},{11... | collective-permute-start | bytes 122888 | tf_op jit(solution)/shard_map/ppermute | solution.py:38
  44.2 1.9 %collective-permute-start.10 = (bf16[8,1,10,256]{3,2,1,0:T(8,128)(2,1)S(1)}, bf16[8,1,10,256]{3,2,1,0:T(8,128)(2,1)S(1)}, u32[]{:S(2)}, u32[]{:S(2)}) collective-permute-start(bf16[8,1,10,256]{3,2,1,0:T(8,128)(2,1)S(1)} %get-tuple-element.26), channel_id=1, source_target_pairs={{1,0},{2,1},{3,2},{4,3},{5,4},{6,5},{7,6},{9,8},{10,9},{11,10},{12... | collective-permute-start | bytes 122888 | tf_op jit(solution)/shard_map/ppermute | solution.py:40
  46.2 3.5 %collective-permute-done.10 = bf16[8,1,10,256]{3,2,1,0:T(8,128)(2,1)S(1)} collective-permute-done((bf16[8,1,10,256]{3,2,1,0:T(8,128)(2,1)S(1)}, bf16[8,1,10,256]{3,2,1,0:T(8,128)(2,1)S(1)}, u32[]{:S(2)}, u32[]{:S(2)}) %collective-permute-start.10) | collective-permute-done | bytes 40992 | tf_op jit(solution)/shard_map/ppermute | solution.py:40
  49.8 0.3 maximum_maximum_fusion
  50.6 0.2 convolution_add_fusion.7
  50.8 0.2 convolution_add_fusion.6
  51.0 0.2 fusion.3
  51.2 0.2 fusion.2
  51.4 0.2 convolution_add_fusion.3
  51.6 0.8 %fusion.7 = bf16[256,256]{1,0:T(8,128)(2,1)} fusion(f32[256,256]{1,0:T(8,128)S(1)} %convolution_add_fusion.3, bf16[256,256]{1,0:T(8,128)(2,1)S(1)} %bitcast.200, bf16[3,3,256,256]{3,2,1,0:T(8,128)(2,1)S(1)} %copy-done.3), kind=kOutput, calls=%fused_computation.31 | convolution fusion | flops 33685504 | bytes 655360 | tf_op jit(solution)/shard_map/dot_general | solution.py:53
  (56 shorter events, 3.2 us)
Async XLA Ops:
  0.0 28.0 %copy-start = (bf16[256,256]{1,0:T(8,128)(2,1)S(1)}, bf16[256,256]{1,0:T(8,128)(2,1)}, u32[]{:S(2)}) copy-start(bf16[256,256]{1,0:T(8,128)(2,1)} %param.18) | copy-start | bytes 393220
  0.0 8.7 %copy-start.2 = (bf16[3,3,256,256]{3,2,1,0:T(8,128)(2,1)S(1)}, bf16[3,3,256,256]{3,2,1,0:T(8,128)(2,1)}, u32[]{:S(2)}) copy-start(bf16[3,3,256,256]{3,2,1,0:T(8,128)(2,1)} %param.12) | copy-start | bytes 3538948
  0.9 5.7 %collective-permute-start.1 = (bf16[2,1,32,256]{3,2,1,0:T(8,128)(2,1)S(1)}, bf16[2,1,32,256]{3,2,1,0:T(8,128)(2,1)S(1)}, u32[]{:S(2)}, u32[]{:S(2)}) collective-permute-start(bf16[2,1,32,256]{3,2,1,0:T(8,128)(2,1)S(1)} %get-tuple-element.42), channel_id=1, source_target_pairs={{1,0},{2,1},{3,2},{4,3},{5,4},{6,5},{7,6},{9,8},{10,9},{11,10},{12... | collective-permute-start | bytes 98312 | tf_op jit(solution)/shard_map/ppermute | solution.py:40
  3.5 4.1 %collective-permute-start = (bf16[2,1,32,256]{3,2,1,0:T(8,128)(2,1)S(1)}, bf16[2,1,32,256]{3,2,1,0:T(8,128)(2,1)S(1)}, u32[]{:S(2)}, u32[]{:S(2)}) collective-permute-start(bf16[2,1,32,256]{3,2,1,0:T(8,128)(2,1)S(1)} %get-tuple-element.41), channel_id=1, source_target_pairs={{0,1},{1,2},{2,3},{3,4},{4,5},{5,6},{6,7},{8,9},{9,10},{10,11},{11... | collective-permute-start | bytes 98312 | tf_op jit(solution)/shard_map/ppermute | solution.py:38
  8.6 0.9 %copy-start.1 = (bf16[2,4,32,256]{3,2,1,0:T(8,128)(2,1)S(1)}, bf16[2,4,32,256]{3,2,1,0:T(8,128)(2,1)}, u32[]{:S(2)}) copy-start(bf16[2,4,32,256]{3,2,1,0:T(8,128)(2,1)} %param.11) | copy-start | bytes 393220
  10.9 7.5 %copy-start.4 = (bf16[3,3,256,256]{3,2,1,0:T(8,128)(2,1)S(1)}, bf16[3,3,256,256]{3,2,1,0:T(8,128)(2,1)}, u32[]{:S(2)}) copy-start(bf16[3,3,256,256]{3,2,1,0:T(8,128)(2,1)} %param.13) | copy-start | bytes 3538948
  11.0 6.4 %collective-permute-start.3 = (bf16[2,1,32,256]{3,2,1,0:T(8,128)(2,1)S(1)}, bf16[2,1,32,256]{3,2,1,0:T(8,128)(2,1)S(1)}, u32[]{:S(2)}, u32[]{:S(2)}) collective-permute-start(bf16[2,1,32,256]{3,2,1,0:T(8,128)(2,1)S(1)} %get-tuple-element.38), channel_id=1, source_target_pairs={{1,0},{2,1},{3,2},{4,3},{5,4},{6,5},{7,6},{9,8},{10,9},{11,10},{12... | collective-permute-start | bytes 98312 | tf_op jit(solution)/shard_map/ppermute | solution.py:40
  14.2 4.1 %collective-permute-start.2 = (bf16[2,1,32,256]{3,2,1,0:T(8,128)(2,1)S(1)}, bf16[2,1,32,256]{3,2,1,0:T(8,128)(2,1)S(1)}, u32[]{:S(2)}, u32[]{:S(2)}) collective-permute-start(bf16[2,1,32,256]{3,2,1,0:T(8,128)(2,1)S(1)} %get-tuple-element.37), channel_id=1, source_target_pairs={{0,1},{1,2},{2,3},{3,4},{4,5},{5,6},{6,7},{8,9},{9,10},{10,11},{11... | collective-permute-start | bytes 98312 | tf_op jit(solution)/shard_map/ppermute | solution.py:38
  19.9 3.0 %copy-start.9 = (f32[8,8]{1,0:T(8,128)S(1)}, f32[8,8]{1,0:T(8,128)}, u32[]{:S(2)}) copy-start(f32[8,8]{1,0:T(8,128)} %param.20) | copy-start | bytes 772
  20.1 7.1 %copy-start.5 = (bf16[3,256,256]{2,1,0:T(8,128)(2,1)S(1)}, bf16[3,256,256]{2,1,0:T(8,128)(2,1)}, u32[]{:S(2)}) copy-start(bf16[3,256,256]{2,1,0:T(8,128)(2,1)} %param.14) | copy-start | bytes 1179652
  20.4 2.8 %collective-permute-start.6 = (bf16[2,4,8,256]{3,2,1,0:T(8,128)(2,1)S(1)}, bf16[2,4,8,256]{3,2,1,0:T(8,128)(2,1)S(1)}, u32[]{:S(2)}, u32[]{:S(2)}) collective-permute-start(bf16[2,4,8,256]{3,2,1,0:T(8,128)(2,1)S(1)} %get-tuple-element.32), channel_id=1, source_target_pairs={{0,24},{8,0},{16,8},{24,16},{1,25},{9,1},{17,9},{25,17},{2,26},{10... | collective-permute-start | bytes 98312 | tf_op jit(solution)/shard_map/ppermute | solution.py:25
  21.6 2.8 %collective-permute-start.5 = (bf16[2,4,8,256]{3,2,1,0:T(8,128)(2,1)S(1)}, bf16[2,4,8,256]{3,2,1,0:T(8,128)(2,1)S(1)}, u32[]{:S(2)}, u32[]{:S(2)}) collective-permute-start(bf16[2,4,8,256]{3,2,1,0:T(8,128)(2,1)S(1)} %get-tuple-element.33), channel_id=1, source_target_pairs={{0,16},{8,24},{16,0},{24,8},{1,17},{9,25},{17,1},{25,9},{2,18},{10... | collective-permute-start | bytes 98312 | tf_op jit(solution)/shard_map/ppermute | solution.py:25
  22.9 3.7 %collective-permute-start.4 = (bf16[2,4,8,256]{3,2,1,0:T(8,128)(2,1)S(1)}, bf16[2,4,8,256]{3,2,1,0:T(8,128)(2,1)S(1)}, u32[]{:S(2)}, u32[]{:S(2)}) collective-permute-start(bf16[2,4,8,256]{3,2,1,0:T(8,128)(2,1)S(1)} %get-tuple-element.34), channel_id=1, source_target_pairs={{0,8},{8,16},{16,24},{24,0},{1,9},{9,17},{17,25},{25,1},{2,10},{10... | collective-permute-start | bytes 98312 | tf_op jit(solution)/shard_map/ppermute | solution.py:25
  26.6 1.3 %copy-start.10 = (f32[256]{0:T(256)S(1)}, f32[256]{0:T(256)}, u32[]{:S(2)}) copy-start(f32[256]{0:T(256)} %param.15) | copy-start | bytes 3076
  27.4 0.9 %copy-start.6 = (bf16[256,256]{1,0:T(8,128)(2,1)S(1)}, bf16[256,256]{1,0:T(8,128)(2,1)}, u32[]{:S(2)}) copy-start(bf16[256,256]{1,0:T(8,128)(2,1)} %param.17) | copy-start | bytes 393220
  27.6 0.9 %copy-start.7 = (bf16[256,256]{1,0:T(8,128)(2,1)S(1)}, bf16[256,256]{1,0:T(8,128)(2,1)}, u32[]{:S(2)}) copy-start(bf16[256,256]{1,0:T(8,128)(2,1)} %param.16) | copy-start | bytes 393220
  28.3 1.0 %copy-start.8 = (bf16[256,256]{1,0:T(8,128)(2,1)S(1)}, bf16[256,256]{1,0:T(8,128)(2,1)}, u32[]{:S(2)}) copy-start(bf16[256,256]{1,0:T(8,128)(2,1)} %param.19) | copy-start | bytes 393220
  28.7 6.2 %copy-start.3 = (bf16[3,3,256,256]{3,2,1,0:T(8,128)(2,1)S(1)}, bf16[3,3,256,256]{3,2,1,0:T(8,128)(2,1)}, u32[]{:S(2)}) copy-start(bf16[3,3,256,256]{3,2,1,0:T(8,128)(2,1)} %param.21) | copy-start | bytes 3538948
  29.6 5.5 %collective-permute-start.8 = (bf16[8,4,1,256]{3,2,1,0:T(2,128)(2,1)S(1)}, bf16[8,4,1,256]{3,2,1,0:T(2,128)(2,1)S(1)}, u32[]{:S(2)}, u32[]{:S(2)}) collective-permute-start(bf16[8,4,1,256]{3,2,1,0:T(2,128)(2,1)S(1)} %get-tuple-element.30), channel_id=1, source_target_pairs={{8,0},{16,8},{24,16},{9,1},{17,9},{25,17},{10,2},{18,10},{26,18},{... | collective-permute-start | bytes 49160 | tf_op jit(solution)/shard_map/ppermute | solution.py:40
  31.5 5.6 %collective-permute-start.7 = (bf16[8,4,1,256]{3,2,1,0:T(2,128)(2,1)S(1)}, bf16[8,4,1,256]{3,2,1,0:T(2,128)(2,1)S(1)}, u32[]{:S(2)}, u32[]{:S(2)}) collective-permute-start(bf16[8,4,1,256]{3,2,1,0:T(2,128)(2,1)S(1)} %get-tuple-element.29), channel_id=1, source_target_pairs={{0,8},{8,16},{16,24},{1,9},{9,17},{17,25},{2,10},{10,18},{18,26},{... | collective-permute-start | bytes 49160 | tf_op jit(solution)/shard_map/ppermute | solution.py:38
  37.2 9.0 %collective-permute-start.9 = (bf16[8,1,10,256]{3,2,1,0:T(8,128)(2,1)S(1)}, bf16[8,1,10,256]{3,2,1,0:T(8,128)(2,1)S(1)}, u32[]{:S(2)}, u32[]{:S(2)}) collective-permute-start(bf16[8,1,10,256]{3,2,1,0:T(8,128)(2,1)S(1)} %get-tuple-element.25), channel_id=1, source_target_pairs={{0,1},{1,2},{2,3},{3,4},{4,5},{5,6},{6,7},{8,9},{9,10},{10,11},{11... | collective-permute-start | bytes 122888 | tf_op jit(solution)/shard_map/ppermute | solution.py:38
  44.2 5.6 %collective-permute-start.10 = (bf16[8,1,10,256]{3,2,1,0:T(8,128)(2,1)S(1)}, bf16[8,1,10,256]{3,2,1,0:T(8,128)(2,1)S(1)}, u32[]{:S(2)}, u32[]{:S(2)}) collective-permute-start(bf16[8,1,10,256]{3,2,1,0:T(8,128)(2,1)S(1)} %get-tuple-element.26), channel_id=1, source_target_pairs={{1,0},{2,1},{3,2},{4,3},{5,4},{6,5},{7,6},{9,8},{10,9},{11,10},{12... | collective-permute-start | bytes 122888 | tf_op jit(solution)/shard_map/ppermute | solution.py:40
